TPU v7x, 128 devices: a whole 4x4x4 slice. The times are simulated.
128 devices in a mesh: group: 8 (over y, core), local: 16 (over z, x).
Axes of the slice: x: 4, y: 4, z: 4, core: 2. Of those that a mesh axis runs over, the one named last changes fastest.
Arguments:
- lookup_grads: bfloat16 [1048576, 256], P(('group', 'local')), may hold values from -0.29882812 to 0.29882812
- slot_index: int32 [2, 1048576], P(None, ('group', 'local')), may hold values from 0 to 2047, as said below
- unique_rows: int32 [2, 16384], P(None, ('group', 'local')), may hold values from -1 to 131071, as said below
- tables: float32 [2, 131072, 256], P(None, ('group', 'local')), may hold values from -6 to 6
- accums: float32 [2, 131072], P(None, ('group', 'local')), may hold values from 0.01 to 1
Outputs:
- new_tables: float32 [2, 131072, 256], P(None, ('group', 'local'))
- new_accums: float32 [2, 131072], P(None, ('group', 'local'))
Inputs may be any that keep to these rules, and one draw needn't show every extreme that they name: slot_index[t, i] names a slot of lookup i's group list whose entry in unique_rows[t] is not -1. `unique_rows`: table row p is owned by device p // 1024, which is device (group p // 16384, local p // 1024 % 16). Group g's list is entries g * 2048 to (g + 1) * 2048 - 1; its block l of 128 entries consists of 8 buckets of 16 entries, bucket h holding only rows owned by device (group h, local l), the used entries first and -1 after them. Rows within a group's list are distinct. In every draw and table some device (group h, local l) gets a full bucket from every group.
All inputs are finite; a program needn't handle non-finite values.
Results may differ from a plain program's by a relative error of at most 0.0003.
Values sent between devices are 32-bit elements; how exact they have to be, the bound alone decides.
No kernel may reach another device: no remote copies, remote signals or barrier semaphores. Data moves between devices by JAX's collectives and lax.ppermute only.
A program may use at most 64 MiB of HBM per device.

v0:
```python
import jax
import jax.numpy as jnp
from jax import lax
from jax.sharding import PartitionSpec as P

learning_rate = 0.1
epsilon = 1e-08


def slot_sums(lookup_grads, slot_index, row_count):
    block_len = min(2048, lookup_grads.shape[0])
    block_count = lookup_grads.shape[0] // block_len
    width = lookup_grads.shape[1]
    grad_blocks = lookup_grads.reshape(block_count, block_len, width)
    index_blocks = jnp.transpose(slot_index.reshape(2, block_count, block_len), (1, 0, 2))
    targets = lax.iota(jnp.int32, row_count)

    def accumulate(running, inputs):
        gradients, indices = inputs
        pieces = []
        for table_index in range(2):
            onehot = (indices[table_index][:, None] == targets[None, :]).astype(jnp.bfloat16)
            pieces.append(
                lax.dot_general(
                    onehot, gradients, (((0,), (0,)), ((), ())), preferred_element_type=jnp.float32
                )
            )
        return (running + jnp.concatenate(pieces, axis=1), None)

    start_sums = jnp.zeros((row_count, 2 * width), jnp.float32)
    summed, _ = lax.scan(accumulate, start_sums, (grad_blocks, index_blocks))
    return summed


def apply_update(summed, row_pairs, tables, accums):
    rows_dev = tables.shape[1]
    width = tables.shape[2]
    new_tables = []
    new_accums = []
    for table_index in range(2):
        row_numbers = row_pairs[:, table_index]
        local_rows = jnp.where(row_numbers < 0, rows_dev, row_numbers % rows_dev)
        values = summed[:, table_index * width : (table_index + 1) * width]
        row_grads = (
            jnp.zeros((rows_dev, width), jnp.float32).at[local_rows].add(values, mode="drop")
        )
        accum_new = accums[table_index] + jnp.mean(row_grads * row_grads, axis=1)
        table_new = tables[table_index] - learning_rate * row_grads / (
            jnp.sqrt(accum_new)[:, None] + epsilon
        )
        new_tables.append(table_new)
        new_accums.append(accum_new)
    return (jnp.stack(new_tables), jnp.stack(new_accums))


def local(lookup_grads, slot_index, unique_rows, tables, accums):
    n_group = lax.axis_size("group")
    n_local = lax.axis_size("local")
    slots = unique_rows.shape[1]
    capacity = slots // n_group
    width = lookup_grads.shape[1]
    row_pairs = jnp.transpose(unique_rows)
    own_sums = slot_sums(lookup_grads, slot_index, slots * n_local)
    ordered = own_sums.reshape(n_local, n_group, capacity, 2 * width)
    ordered = jnp.transpose(ordered, (1, 0, 2, 3)).reshape(n_local * slots, 2 * width)
    received = lax.all_to_all(ordered, ("group", "local"), split_axis=0, concat_axis=0, tiled=True)
    arrived = jnp.sum(received.reshape(n_group, n_local, capacity, 2 * width), axis=1).reshape(
        slots, 2 * width
    )
    arrived_rows = lax.all_to_all(row_pairs, "group", split_axis=0, concat_axis=0, tiled=True)
    return apply_update(arrived, arrived_rows, tables, accums)


def solution(mesh):
    return jax.shard_map(
        local,
        mesh=mesh,
        in_specs=(
            P(("group", "local"), None),
            P(None, ("group", "local")),
            P(None, ("group", "local")),
            P(None, ("group", "local"), None),
            P(None, ("group", "local")),
        ),
        out_specs=(P(None, ("group", "local"), None), P(None, ("group", "local"))),
        check_vma=False,
    )
```

profile of v0, /device:TPU:1, one launch (start us, length us, event | category | flops | bytes accessed | tf_op | source)
XLA Modules:
  0.0 159.0 jit_solution(276250633649171804)
XLA Ops:
  0.6 0.8 all_to_all.14
  1.4 0.6 copy.11
  2.0 6.0 %all-to-all-start = ((s32[8,16,2]{1,2,0:T(2,128)}), s32[8,16,2]{1,2,0:T(2,128)S(1)}, u32[]{:S(2)}, u32[]{:S(2)}) async-start(s32[8,16,2]{1,2,0:T(2,128)} %copy.11), calls=%async_computation | async-start | bytes 16384 | tf_op jit(solution)/shard_map/all_to_all | solution.py:70
  8.0 68.6 %while.12 = (s32[]{:T(128)}, f32[2048,512]{0,1:T(8,128)}, s32[4,2,2048]{2,1,0:T(2,128)}, bf16[4,2048,256]{2,1,0:T(8,128)(2,1)}, s32[]{:T(128)}, /*index=5*/s32[]{:T(128)}, s32[]{}) while((s32[]{:T(128)}, f32[2048,512]{0,1:T(8,128)}, s32[4,2,2048]{2,1,0:T(2,128)}, bf16[4,2048,256]{2,1,0:T(8,128)(2,1)}, s32[]{:T(128)}, ...), condition=%wide.region_1.2_spmd.clone.clone, body=%wide.region_0.1_spmd.clone.clone.sunk | while | flops 4306501632 | bytes 18924652 | solution.py:31
  8.0 0.8 constant_dynamic-slice_fusion.3
  8.8 4.8 %fusion.30 = f32[2048,256]{0,1:T(8,128)S(1)} fusion(s32[2048]{0:T(1024)S(1)} %bitcast.56, bf16[4,2048,256]{2,1,0:T(8,128)(2,1)} %get-tuple-element.130, s32[]{:T(128)} %get-tuple-element.120), kind=kOutput, calls=%fused_computation.6.clone.1 | convolution fusion | flops 2151677952 | bytes 3154432 | tf_op jit(solution)/shard_map/while/body/eval_jaxpr/dot_general | solution.py:24
  13.6 6.1 %fusion.31 = f32[2048,256]{0,1:T(8,128)} fusion(s32[2048]{0:T(1024)S(1)} %bitcast.55, bf16[4,2048,256]{2,1,0:T(8,128)(2,1)} %get-tuple-element.130, s32[]{:T(128)} %get-tuple-element.120), kind=kOutput, calls=%fused_computation.5.clone.1 | convolution fusion | flops 2151677952 | bytes 3154432 | tf_op jit(solution)/shard_map/while/body/eval_jaxpr/dot_general | solution.py:24
  19.7 4.5 %maximum_add_fusion.2 = f32[2048,512]{0,1:T(8,128)} fusion(f32[2048,256]{0,1:T(8,128)S(1)} %fusion.30, f32[2048,256]{0,1:T(8,128)} %fusion.31, f32[2048,512]{0,1:T(8,128)} %get-tuple-element.121, pred[]{:T(512)S(6)} %compare.5), kind=kLoop, calls=%fused_computation.9.clone.1 | loop fusion | flops 3145728 | bytes 12582913 | tf_op jit(solution)/shard_map/while/body/eval_jaxpr/add | solution.py:28
  24.2 0.8 constant_dynamic-slice_fusion.3
  25.0 4.8 %fusion.30 = f32[2048,256]{0,1:T(8,128)S(1)} fusion(s32[2048]{0:T(1024)S(1)} %bitcast.56, bf16[4,2048,256]{2,1,0:T(8,128)(2,1)} %get-tuple-element.130, s32[]{:T(128)} %get-tuple-element.120), kind=kOutput, calls=%fused_computation.6.clone.1 | convolution fusion | flops 2151677952 | bytes 3154432 | tf_op jit(solution)/shard_map/while/body/eval_jaxpr/dot_general | solution.py:24
  29.8 6.1 %fusion.31 = f32[2048,256]{0,1:T(8,128)} fusion(s32[2048]{0:T(1024)S(1)} %bitcast.55, bf16[4,2048,256]{2,1,0:T(8,128)(2,1)} %get-tuple-element.130, s32[]{:T(128)} %get-tuple-element.120), kind=kOutput, calls=%fused_computation.5.clone.1 | convolution fusion | flops 2151677952 | bytes 3154432 | tf_op jit(solution)/shard_map/while/body/eval_jaxpr/dot_general | solution.py:24
  35.9 5.8 %maximum_add_fusion.2 = f32[2048,512]{0,1:T(8,128)} fusion(f32[2048,256]{0,1:T(8,128)S(1)} %fusion.30, f32[2048,256]{0,1:T(8,128)} %fusion.31, f32[2048,512]{0,1:T(8,128)} %get-tuple-element.121, pred[]{:T(512)S(6)} %compare.5), kind=kLoop, calls=%fused_computation.9.clone.1 | loop fusion | flops 3145728 | bytes 12582913 | tf_op jit(solution)/shard_map/while/body/eval_jaxpr/add | solution.py:28
  41.6 0.8 constant_dynamic-slice_fusion.3
  42.5 4.8 %fusion.30 = f32[2048,256]{0,1:T(8,128)S(1)} fusion(s32[2048]{0:T(1024)S(1)} %bitcast.56, bf16[4,2048,256]{2,1,0:T(8,128)(2,1)} %get-tuple-element.130, s32[]{:T(128)} %get-tuple-element.120), kind=kOutput, calls=%fused_computation.6.clone.1 | convolution fusion | flops 2151677952 | bytes 3154432 | tf_op jit(solution)/shard_map/while/body/eval_jaxpr/dot_general | solution.py:24
  47.2 6.1 %fusion.31 = f32[2048,256]{0,1:T(8,128)} fusion(s32[2048]{0:T(1024)S(1)} %bitcast.55, bf16[4,2048,256]{2,1,0:T(8,128)(2,1)} %get-tuple-element.130, s32[]{:T(128)} %get-tuple-element.120), kind=kOutput, calls=%fused_computation.5.clone.1 | convolution fusion | flops 2151677952 | bytes 3154432 | tf_op jit(solution)/shard_map/while/body/eval_jaxpr/dot_general | solution.py:24
  53.3 5.8 %maximum_add_fusion.2 = f32[2048,512]{0,1:T(8,128)} fusion(f32[2048,256]{0,1:T(8,128)S(1)} %fusion.30, f32[2048,256]{0,1:T(8,128)} %fusion.31, f32[2048,512]{0,1:T(8,128)} %get-tuple-element.121, pred[]{:T(512)S(6)} %compare.5), kind=kLoop, calls=%fused_computation.9.clone.1 | loop fusion | flops 3145728 | bytes 12582913 | tf_op jit(solution)/shard_map/while/body/eval_jaxpr/add | solution.py:28
  59.1 0.8 constant_dynamic-slice_fusion.3
  59.9 4.8 %fusion.30 = f32[2048,256]{0,1:T(8,128)S(1)} fusion(s32[2048]{0:T(1024)S(1)} %bitcast.56, bf16[4,2048,256]{2,1,0:T(8,128)(2,1)} %get-tuple-element.130, s32[]{:T(128)} %get-tuple-element.120), kind=kOutput, calls=%fused_computation.6.clone.1 | convolution fusion | flops 2151677952 | bytes 3154432 | tf_op jit(solution)/shard_map/while/body/eval_jaxpr/dot_general | solution.py:24
  64.7 6.1 %fusion.31 = f32[2048,256]{0,1:T(8,128)} fusion(s32[2048]{0:T(1024)S(1)} %bitcast.55, bf16[4,2048,256]{2,1,0:T(8,128)(2,1)} %get-tuple-element.130, s32[]{:T(128)} %get-tuple-element.120), kind=kOutput, calls=%fused_computation.5.clone.1 | convolution fusion | flops 2151677952 | bytes 3154432 | tf_op jit(solution)/shard_map/while/body/eval_jaxpr/dot_general | solution.py:24
  70.8 5.8 %maximum_add_fusion.2 = f32[2048,512]{0,1:T(8,128)} fusion(f32[2048,256]{0,1:T(8,128)S(1)} %fusion.30, f32[2048,256]{0,1:T(8,128)} %fusion.31, f32[2048,512]{0,1:T(8,128)} %get-tuple-element.121, pred[]{:T(512)S(6)} %compare.5), kind=kLoop, calls=%fused_computation.9.clone.1 | loop fusion | flops 3145728 | bytes 12582913 | tf_op jit(solution)/shard_map/while/body/eval_jaxpr/add | solution.py:28
  76.6 5.3 %copy.13 = f32[2048,512]{1,0:T(8,128)} copy(f32[2048,512]{0,1:T(8,128)} %get-tuple-element.32) | data formatting | bytes 8388608 | tf_op jit(solution)/shard_map/while | solution.py:31
  81.9 5.0 %copy.14 = f32[8,16,16,512]{3,2,1,0:T(8,128)} copy(f32[8,16,16,512]{3,2,0,1:T(8,128)} %bitcast.52) | data formatting | bytes 8388608 | tf_op jit(solution)/shard_map/transpose | solution.py:65
  86.9 0.0 all-to-all-done
  86.9 10.8 %all-to-all-start.1 = ((f32[128,16,512]{2,1,0:T(8,128)}), f32[128,16,512]{2,1,0:T(8,128)}, u32[]{:S(2)}, u32[]{:S(2)}) async-start(f32[128,16,512]{2,1,0:T(8,128)} %bitcast.51), calls=%async_computation.1 | async-start | bytes 8388608 | tf_op jit(solution)/shard_map/all_to_all | solution.py:66
  97.7 0.1 all_to_all.16
  97.8 0.0 copy-start
  97.8 51.1 %all-to-all-done.1 = f32[128,16,512]{2,1,0:T(8,128)} async-done(((f32[128,16,512]{2,1,0:T(8,128)}), f32[128,16,512]{2,1,0:T(8,128)}, u32[]{:S(2)}, u32[]{:S(2)}) %all-to-all-start.1) | async-done | bytes 4194336 | tf_op jit(solution)/shard_map/all_to_all | solution.py:66
  148.8 2.6 %bitcast_reduce_fusion = f32[8,16,512]{2,1,0:T(8,128)S(1)} fusion(f32[128,16,512]{2,1,0:T(8,128)} %all-to-all-done.1), kind=kLoop, calls=%fused_computation.18 | loop fusion | flops 983040 | bytes 4456448 | tf_op jit(solution)/shard_map/reduce_sum | solution.py:67
  151.5 1.5 scatter_custom_fusion
  153.0 0.2 multiply_reduce_fusion.1
  153.2 1.5 scatter_custom_fusion.1
  154.8 0.2 multiply_reduce_fusion
  155.0 0.0 copy-done
  155.0 1.9 %fusion.13 = (f32[1,1024,256]{2,1,0:T(8,128)S(1)}, f32[1,1024,256]{2,1,0:T(8,128)S(1)}) fusion(f32[1024,256]{1,0:T(8,128)S(1)} %scatter_custom_fusion, f32[2,1024,256]{2,1,0:T(8,128)} %param.10, f32[1024]{0:T(1024)S(1)} %get-tuple-element.83, f32[1024]{0:T(1024)S(1)} %get-tuple-element.82, f32[1024,256]{1,0:T(8,128)S(1)} %scatter_custom_fusion.1), kind=kLoop, calls=%fused_computation.23 | loop fusion | flops 1572864 | bytes 6299648 | tf_op jit(solution)/shard_map/stack | solution.py:53
  156.9 1.5 pad_maximum_fusion
  158.4 0.6 pad_maximum_fusion.1
  (7 shorter events, 0.1 us)
Async XLA Ops:
  2.0 84.9 %all-to-all-start = ((s32[8,16,2]{1,2,0:T(2,128)}), s32[8,16,2]{1,2,0:T(2,128)S(1)}, u32[]{:S(2)}, u32[]{:S(2)}) async-start(s32[8,16,2]{1,2,0:T(2,128)} %copy.11), calls=%async_computation | async-start | bytes 16384 | tf_op jit(solution)/shard_map/all_to_all | solution.py:70
  86.9 62.0 %all-to-all-start.1 = ((f32[128,16,512]{2,1,0:T(8,128)}), f32[128,16,512]{2,1,0:T(8,128)}, u32[]{:S(2)}, u32[]{:S(2)}) async-start(f32[128,16,512]{2,1,0:T(8,128)} %bitcast.51), calls=%async_computation.1 | async-start | bytes 8388608 | tf_op jit(solution)/shard_map/all_to_all | solution.py:66
  97.8 57.2 %copy-start = (f32[2,1024]{1,0:T(2,128)S(1)}, f32[2,1024]{1,0:T(2,128)}, u32[]{:S(2)}) copy-start(f32[2,1024]{1,0:T(2,128)} %param.11) | copy-start | bytes 24580
where the time goes:
time: 160 us; the launch traced here: 159 us
  waiting for transfers between devices  51.1 us (32%)
  matrix products  43.5 us (27%)
  other arithmetic  31.9 us (20%)
  starting transfers between devices  16.8 us (10%)
  local copies, waits for them, and re-layouts  15 us (9%)
    all_to_all x1, waiting for transfers between devices, local(): lax.all_to_all(ordered, ('group', 'local'), split_axis=0, concat_axis=0,...  51.1 us
    dot_general x8, matrix products, accumulate(): lax.dot_general(onehot, gradients, (((0,), (0,)), ((), ())), preferred_el...  43.5 us
    add x4, other arithmetic, accumulate(): return (running + jnp.concatenate(pieces, axis=1), None)  21.8 us
    all_to_all x1, starting transfers between devices, local(): lax.all_to_all(ordered, ('group', 'local'), split_axis=0, concat_axis=0,...  10.8 us
    all_to_all x1, starting transfers between devices, local(): lax.all_to_all(row_pairs, 'group', split_axis=0, concat_axis=0, tiled=True)  5.97 us
    while x1, local copies, waits for them, and re-layouts, slot_sums(): summed, _ = lax.scan(accumulate, start_sums, (grad_blocks, index_blocks))  5.34 us
    transpose x1, local copies, waits for them, and re-layouts, local(): jnp.transpose(ordered, (1, 0, 2, 3)).reshape(n_local * slots, 2 * width)  4.95 us
    another operation x3, other arithmetic, apply_update(): return (jnp.stack(new_tables), jnp.stack(new_accums))  3.95 us
  transfers between devices with their start and end apart: 2, of which 1 were waited for; matrix products, arithmetic and copies ran while one was open for 50% of the time, Pallas kernels for 0%

commit v1 on v0

--- a/solution.py
+++ b/solution.py
@@ -67,7 +67,19 @@
     arrived = jnp.sum(received.reshape(n_group, n_local, capacity, 2 * width), axis=1).reshape(
         slots, 2 * width
     )
-    arrived_rows = lax.all_to_all(row_pairs, "group", split_axis=0, concat_axis=0, tiled=True)
+    ways, here = (lax.axis_size("group"), lax.axis_index("group"))
+    width_2 = row_pairs.shape[0] // ways
+    lengths = list(row_pairs.shape)
+    lengths[0] = width_2
+    height = lengths[0]
+    lengths[0] = height * ways
+    full = jnp.zeros(lengths, row_pairs.dtype)
+    for mask in range(ways):
+        part = lax.dynamic_slice_in_dim(row_pairs, (here ^ mask) * width_2, width_2, axis=0)
+        if mask:
+            part = lax.ppermute(part, "group", [(d, d ^ mask) for d in range(ways)])
+        full = lax.dynamic_update_slice_in_dim(full, part, (here ^ mask) * height, axis=0)
+    arrived_rows = full
     return apply_update(arrived, arrived_rows, tables, accums)
 
 

time: 160 us -> 141 us (0.88)
  other arithmetic: 31.9 us -> 16.1 us
  waiting for transfers between devices: 51.1 us -> 40.9 us
  local copies, waits for them, and re-layouts: 15 us -> 23.2 us
  matrix products: 43.5 us -> 38.8 us
  starting transfers between devices: 16.8 us -> 20.5 us
    all_to_all x1, waiting for transfers between devices: 51.1 us -> 0.59 us  [local(): lax.all_to_all(ordered, ('group', 'local'), split_axis=0, concat_axis=0,...]
    ppermute x0 -> x7, waiting for transfers between devices: none -> 40.3 us  [local(): part = lax.ppermute(part, 'group', [(d, d ^ mask) for d in range(ways)])]
    add x4, other arithmetic: 21.8 us -> 5.96 us  [accumulate(): return (running + jnp.concatenate(pieces, axis=1), None)]
    ppermute x0 -> x7, starting transfers between devices: none -> 8.52 us  [local(): part = lax.ppermute(part, 'group', [(d, d ^ mask) for d in range(ways)])]
    while x0 -> x16, local copies, waits for them, and re-layouts: none -> 7.9 us
    all_to_all x1 -> x0, starting transfers between devices: 5.97 us -> none  [local(): lax.all_to_all(row_pairs, 'group', split_axis=0, concat_axis=0, tiled=True)]
    dot_general x8, matrix products: 43.5 us -> 38.8 us  [accumulate(): lax.dot_general(onehot, gradients, (((0,), (0,)), ((), ())), preferred_el...]
  transfers between devices with their start and end apart: 2 -> 8, of which waited for: 1 -> 5; matrix products, arithmetic and copies ran while one was open for 50% -> 1% of each run, Pallas kernels for 0% -> 0%
where the time goes in v1:
time: 141 us; the launch traced here: 140 us
  waiting for transfers between devices  40.9 us (29%)
  matrix products  38.8 us (28%)
  local copies, waits for them, and re-layouts  23.2 us (16%)
  starting transfers between devices  20.5 us (15%)
  other arithmetic  16.1 us (11%)
    ppermute x7, waiting for transfers between devices, local(): part = lax.ppermute(part, 'group', [(d, d ^ mask) for d in range(ways)])  40.3 us
    dot_general x8, matrix products, accumulate(): lax.dot_general(onehot, gradients, (((0,), (0,)), ((), ())), preferred_el...  38.8 us
    all_to_all x1, starting transfers between devices, local(): lax.all_to_all(ordered, ('group', 'local'), split_axis=0, concat_axis=0,...  12 us
    ppermute x7, starting transfers between devices, local(): part = lax.ppermute(part, 'group', [(d, d ^ mask) for d in range(ways)])  8.52 us
    while x16, local copies, waits for them, and re-layouts  7.9 us
    add x4, other arithmetic, accumulate(): return (running + jnp.concatenate(pieces, axis=1), None)  5.96 us
    while x1, local copies, waits for them, and re-layouts, slot_sums(): summed, _ = lax.scan(accumulate, start_sums, (grad_blocks, index_blocks))  5.35 us
    transpose x1, local copies, waits for them, and re-layouts, local(): jnp.transpose(ordered, (1, 0, 2, 3)).reshape(n_local * slots, 2 * width)  5 us
  transfers between devices with their start and end apart: 8, of which 5 were waited for; matrix products, arithmetic and copies ran while one was open for 1% of the time, Pallas kernels for 0%

profile of v1, /device:TPU:1, one launch (start us, length us, event | category | flops | bytes accessed | tf_op | source)
XLA Modules:
  0.0 140.4 jit_solution(12140327442248434260)
XLA Ops:
  0.6 56.1 %while.12 = (s32[]{:T(128)}, f32[2048,512]{0,1:T(8,128)}, s32[4,2,2048]{2,1,0:T(2,128)}, bf16[4,2048,256]{2,1,0:T(8,128)(2,1)}, s32[]{:T(128)}, /*index=5*/s32[]{:T(128)}, s32[]{}) while((s32[]{:T(128)}, f32[2048,512]{0,1:T(8,128)}, s32[4,2,2048]{2,1,0:T(2,128)}, bf16[4,2048,256]{2,1,0:T(8,128)(2,1)}, s32[]{:T(128)}, ...), condition=%wide.region_1.2_spmd.clone.clone, body=%wide.region_0.1_spmd.clone.clone.sunk | while | flops 4306501632 | bytes 52478128 | solution.py:31
  0.7 0.8 constant_dynamic-slice_fusion.11
  1.5 4.8 %fusion.39 = f32[2048,256]{0,1:T(8,128)S(1)} fusion(s32[2048]{0:T(1024)S(1)} %bitcast.67, bf16[4,2048,256]{2,1,0:T(8,128)(2,1)} %get-tuple-element.138, s32[]{:T(128)S(6)} %copy.19), kind=kOutput, calls=%fused_computation.5.clone.1 | convolution fusion | flops 2151677952 | bytes 3153924 | tf_op jit(solution)/shard_map/while/body/eval_jaxpr/dot_general | solution.py:24
  6.3 4.9 %fusion.38 = f32[2048,256]{0,1:T(8,128)S(1)} fusion(s32[2048]{0:T(1024)S(1)} %bitcast.66, bf16[4,2048,256]{2,1,0:T(8,128)(2,1)} %get-tuple-element.138, s32[]{:T(128)S(6)} %copy.19), kind=kOutput, calls=%fused_computation.6.clone.1 | convolution fusion | flops 2151677952 | bytes 3153924 | tf_op jit(solution)/shard_map/while/body/eval_jaxpr/dot_general | solution.py:24
  11.2 1.5 %maximum_add_fusion.2 = f32[2048,512]{0,1:T(8,128)S(1)} fusion(f32[2048,256]{0,1:T(8,128)S(1)} %fusion.38, f32[2048,256]{0,1:T(8,128)S(1)} %fusion.39, f32[2048,512]{0,1:T(8,128)S(1)} %copy-done, pred[]{:T(512)S(6)} %compare.5), kind=kLoop, calls=%fused_computation.9.clone.1 | loop fusion | flops 3145728 | bytes 12582913 | tf_op jit(solution)/shard_map/while/body/eval_jaxpr/add | solution.py:28
  12.7 2.0 %copy-done.1 = f32[2048,512]{0,1:T(8,128)} copy-done((f32[2048,512]{0,1:T(8,128)}, f32[2048,512]{0,1:T(8,128)S(1)}, u32[]{:S(2)}) %copy-start.1) | copy-done | bytes 4194328 | tf_op jit(solution)/shard_map/while
  14.7 0.8 constant_dynamic-slice_fusion.11
  15.5 4.8 %fusion.39 = f32[2048,256]{0,1:T(8,128)S(1)} fusion(s32[2048]{0:T(1024)S(1)} %bitcast.67, bf16[4,2048,256]{2,1,0:T(8,128)(2,1)} %get-tuple-element.138, s32[]{:T(128)S(6)} %copy.19), kind=kOutput, calls=%fused_computation.5.clone.1 | convolution fusion | flops 2151677952 | bytes 3153924 | tf_op jit(solution)/shard_map/while/body/eval_jaxpr/dot_general | solution.py:24
  20.3 4.9 %fusion.38 = f32[2048,256]{0,1:T(8,128)S(1)} fusion(s32[2048]{0:T(1024)S(1)} %bitcast.66, bf16[4,2048,256]{2,1,0:T(8,128)(2,1)} %get-tuple-element.138, s32[]{:T(128)S(6)} %copy.19), kind=kOutput, calls=%fused_computation.6.clone.1 | convolution fusion | flops 2151677952 | bytes 3153924 | tf_op jit(solution)/shard_map/while/body/eval_jaxpr/dot_general | solution.py:24
  25.2 1.5 %maximum_add_fusion.2 = f32[2048,512]{0,1:T(8,128)S(1)} fusion(f32[2048,256]{0,1:T(8,128)S(1)} %fusion.38, f32[2048,256]{0,1:T(8,128)S(1)} %fusion.39, f32[2048,512]{0,1:T(8,128)S(1)} %copy-done, pred[]{:T(512)S(6)} %compare.5), kind=kLoop, calls=%fused_computation.9.clone.1 | loop fusion | flops 3145728 | bytes 12582913 | tf_op jit(solution)/shard_map/while/body/eval_jaxpr/add | solution.py:28
  26.7 2.0 %copy-done.1 = f32[2048,512]{0,1:T(8,128)} copy-done((f32[2048,512]{0,1:T(8,128)}, f32[2048,512]{0,1:T(8,128)S(1)}, u32[]{:S(2)}) %copy-start.1) | copy-done | bytes 4194328 | tf_op jit(solution)/shard_map/while
  28.7 0.8 constant_dynamic-slice_fusion.11
  29.5 4.8 %fusion.39 = f32[2048,256]{0,1:T(8,128)S(1)} fusion(s32[2048]{0:T(1024)S(1)} %bitcast.67, bf16[4,2048,256]{2,1,0:T(8,128)(2,1)} %get-tuple-element.138, s32[]{:T(128)S(6)} %copy.19), kind=kOutput, calls=%fused_computation.5.clone.1 | convolution fusion | flops 2151677952 | bytes 3153924 | tf_op jit(solution)/shard_map/while/body/eval_jaxpr/dot_general | solution.py:24
  34.3 4.9 %fusion.38 = f32[2048,256]{0,1:T(8,128)S(1)} fusion(s32[2048]{0:T(1024)S(1)} %bitcast.66, bf16[4,2048,256]{2,1,0:T(8,128)(2,1)} %get-tuple-element.138, s32[]{:T(128)S(6)} %copy.19), kind=kOutput, calls=%fused_computation.6.clone.1 | convolution fusion | flops 2151677952 | bytes 3153924 | tf_op jit(solution)/shard_map/while/body/eval_jaxpr/dot_general | solution.py:24
  39.2 1.5 %maximum_add_fusion.2 = f32[2048,512]{0,1:T(8,128)S(1)} fusion(f32[2048,256]{0,1:T(8,128)S(1)} %fusion.38, f32[2048,256]{0,1:T(8,128)S(1)} %fusion.39, f32[2048,512]{0,1:T(8,128)S(1)} %copy-done, pred[]{:T(512)S(6)} %compare.5), kind=kLoop, calls=%fused_computation.9.clone.1 | loop fusion | flops 3145728 | bytes 12582913 | tf_op jit(solution)/shard_map/while/body/eval_jaxpr/add | solution.py:28
  40.8 2.0 %copy-done.1 = f32[2048,512]{0,1:T(8,128)} copy-done((f32[2048,512]{0,1:T(8,128)}, f32[2048,512]{0,1:T(8,128)S(1)}, u32[]{:S(2)}) %copy-start.1) | copy-done | bytes 4194328 | tf_op jit(solution)/shard_map/while
  42.7 0.8 constant_dynamic-slice_fusion.11
  43.5 4.8 %fusion.39 = f32[2048,256]{0,1:T(8,128)S(1)} fusion(s32[2048]{0:T(1024)S(1)} %bitcast.67, bf16[4,2048,256]{2,1,0:T(8,128)(2,1)} %get-tuple-element.138, s32[]{:T(128)S(6)} %copy.19), kind=kOutput, calls=%fused_computation.5.clone.1 | convolution fusion | flops 2151677952 | bytes 3153924 | tf_op jit(solution)/shard_map/while/body/eval_jaxpr/dot_general | solution.py:24
  48.3 4.9 %fusion.38 = f32[2048,256]{0,1:T(8,128)S(1)} fusion(s32[2048]{0:T(1024)S(1)} %bitcast.66, bf16[4,2048,256]{2,1,0:T(8,128)(2,1)} %get-tuple-element.138, s32[]{:T(128)S(6)} %copy.19), kind=kOutput, calls=%fused_computation.6.clone.1 | convolution fusion | flops 2151677952 | bytes 3153924 | tf_op jit(solution)/shard_map/while/body/eval_jaxpr/dot_general | solution.py:24
  53.3 1.5 %maximum_add_fusion.2 = f32[2048,512]{0,1:T(8,128)S(1)} fusion(f32[2048,256]{0,1:T(8,128)S(1)} %fusion.38, f32[2048,256]{0,1:T(8,128)S(1)} %fusion.39, f32[2048,512]{0,1:T(8,128)S(1)} %copy-done, pred[]{:T(512)S(6)} %compare.5), kind=kLoop, calls=%fused_computation.9.clone.1 | loop fusion | flops 3145728 | bytes 12582913 | tf_op jit(solution)/shard_map/while/body/eval_jaxpr/add | solution.py:28
  54.8 2.0 %copy-done.1 = f32[2048,512]{0,1:T(8,128)} copy-done((f32[2048,512]{0,1:T(8,128)}, f32[2048,512]{0,1:T(8,128)S(1)}, u32[]{:S(2)}) %copy-start.1) | copy-done | bytes 4194328 | tf_op jit(solution)/shard_map/while
  56.7 5.3 %copy.7 = f32[2048,512]{1,0:T(8,128)} copy(f32[2048,512]{0,1:T(8,128)} %get-tuple-element.32) | data formatting | bytes 8388608 | tf_op jit(solution)/shard_map/while | solution.py:31
  62.1 5.0 %copy.8 = f32[8,16,16,512]{3,2,1,0:T(8,128)} copy(f32[8,16,16,512]{3,2,0,1:T(8,128)} %bitcast.63) | data formatting | bytes 8388608 | tf_op jit(solution)/shard_map/transpose | solution.py:65
  67.1 12.0 %all-to-all-start = ((f32[128,16,512]{2,1,0:T(8,128)}), f32[128,16,512]{2,1,0:T(8,128)}, u32[]{:S(2)}, u32[]{:S(2)}) async-start(f32[128,16,512]{2,1,0:T(8,128)} %bitcast.62), calls=%async_computation | async-start | bytes 8388608 | tf_op jit(solution)/shard_map/all_to_all | solution.py:66
  79.2 2.9 %collective-permute-start.6 = (s32[16,2]{0,1:T(2,128)S(1)}, s32[16,2]{0,1:T(2,128)S(1)}, u32[]{:S(2)}, u32[]{:S(2)}) collective-permute-start(s32[16,2]{0,1:T(2,128)S(1)} %get-tuple-element.82), channel_id=1, source_target_pairs={{0,112},{16,96},{32,80},{48,64},{64,48},{80,32},{96,16},{112,0},{1... | collective-permute-start | bytes 392 | tf_op jit(solution)/shard_map/ppermute | solution.py:80
  82.1 0.6 collective-permute-start.4
  82.7 2.4 %collective-permute-start.3 = (s32[16,2]{0,1:T(2,128)S(1)}, s32[16,2]{0,1:T(2,128)S(1)}, u32[]{:S(2)}, u32[]{:S(2)}) collective-permute-start(s32[16,2]{0,1:T(2,128)S(1)} %get-tuple-element.84), channel_id=1, source_target_pairs={{0,64},{16,80},{32,96},{48,112},{64,0},{80,16},{96,32},{112,48},{1... | collective-permute-start | bytes 392 | tf_op jit(solution)/shard_map/ppermute | solution.py:80
  85.1 0.8 collective-permute-start
  86.0 0.2 dynamic_update_slice.24
  86.2 0.6 collective-permute-done
  86.8 1.7 %collective-permute-start.2 = (s32[16,2]{0,1:T(2,128)S(1)}, s32[16,2]{0,1:T(2,128)S(1)}, u32[]{:S(2)}, u32[]{:S(2)}) collective-permute-start(s32[16,2]{0,1:T(2,128)S(1)} %get-tuple-element.85), channel_id=1, source_target_pairs={{0,48},{16,32},{32,16},{48,0},{64,112},{80,96},{96,80},{112,64},{1... | collective-permute-start | bytes 392 | tf_op jit(solution)/shard_map/ppermute | solution.py:80
  88.6 36.4 %collective-permute-done.1 = s32[16,2]{0,1:T(2,128)S(1)} collective-permute-done((s32[16,2]{0,1:T(2,128)S(1)}, s32[16,2]{0,1:T(2,128)S(1)}, u32[]{:S(2)}, u32[]{:S(2)}) %collective-permute-start.1) | collective-permute-done | bytes 160 | tf_op jit(solution)/shard_map/ppermute | solution.py:80
  125.0 0.2 dynamic_update_slice.26
  125.2 0.9 collective-permute-done.2
  126.2 0.2 dynamic_update_slice.27
  126.4 0.3 dynamic_update_slice.28
  126.6 0.3 dynamic_update_slice.29
  126.9 2.3 %collective-permute-done.5 = s32[16,2]{0,1:T(2,128)S(1)} collective-permute-done((s32[16,2]{0,1:T(2,128)S(1)}, s32[16,2]{0,1:T(2,128)S(1)}, u32[]{:S(2)}, u32[]{:S(2)}) %collective-permute-start.5) | collective-permute-done | bytes 160 | tf_op jit(solution)/shard_map/ppermute | solution.py:80
  129.4 0.3 dynamic_update_slice.31
  129.6 0.6 all-to-all-done
  130.2 2.6 %bitcast_reduce_fusion = f32[8,16,512]{2,1,0:T(8,128)S(1)} fusion(f32[128,16,512]{2,1,0:T(8,128)} %all-to-all-done), kind=kLoop, calls=%fused_computation.18 | loop fusion | flops 983040 | bytes 4456448 | tf_op jit(solution)/shard_map/reduce_sum | solution.py:67
  132.9 1.5 %scatter_custom_fusion.1 = f32[1024,256]{1,0:T(8,128)S(1)} fusion(s32[128]{0:T(128)S(1)} %get-tuple-element.81, f32[]{:T(128)} %constant.22.clone.1, f32[128,512]{1,0:T(8,128)S(1)} %bitcast.64), kind=kCustom, calls=%fused_computation.26 | custom fusion | flops 32768 | bytes 1179652 | tf_op jit(solution)/shard_map/scatter-add | solution.py:45
  134.4 0.2 multiply_reduce_fusion
  134.6 1.5 %scatter_custom_fusion = f32[1024,256]{1,0:T(8,128)S(1)} fusion(s32[128]{0:T(128)S(1)} %get-tuple-element.80, f32[]{:T(128)} %constant.22.clone.1, f32[128,512]{1,0:T(8,128)S(1)} %bitcast.65), kind=kCustom, calls=%fused_computation.28 | custom fusion | flops 32768 | bytes 1179652 | tf_op jit(solution)/shard_map/scatter-add | solution.py:45
  136.2 0.2 multiply_reduce_fusion.1
  136.4 0.6 pad_maximum_fusion.1
  137.0 1.9 %fusion.13 = (f32[1,1024,256]{2,1,0:T(8,128)S(1)}, f32[1,1024,256]{2,1,0:T(8,128)S(1)}) fusion(f32[1024,256]{1,0:T(8,128)S(1)} %scatter_custom_fusion, f32[2,1024,256]{2,1,0:T(8,128)} %param.10, f32[1024]{0:T(1024)S(1)} %get-tuple-element.91, f32[1024]{0:T(1024)S(1)} %get-tuple-element.90, f32[1024,256]{1,0:T(8,128)S(1)} %scatter_custom_fusion.1), kind=kLoop, calls=%fused_computation.23 | loop fusion | flops 1572864 | bytes 6299648 | tf_op jit(solution)/shard_map/stack | solution.py:53
  138.9 1.5 %pad_maximum_fusion = f32[2,1024,256]{2,1,0:T(8,128)} fusion(f32[1,1024,256]{2,1,0:T(8,128)S(1)} %get-tuple-element.75, f32[1,1024,256]{2,1,0:T(8,128)S(1)} %get-tuple-element.74), kind=kLoop, calls=%fused_computation.19 | loop fusion | flops 524288 | bytes 4194304 | tf_op jit(solution)/shard_map/stack | solution.py:53
  (31 shorter events, 0.4 us)
Async XLA Ops:
  6.3 4.9 %copy-start = (f32[2048,512]{0,1:T(8,128)S(1)}, f32[2048,512]{0,1:T(8,128)}, u32[]{:S(2)}) copy-start(f32[2048,512]{0,1:T(8,128)} %get-tuple-element.129) | copy-start | bytes 12582916 | tf_op jit(solution)/shard_map/while
  12.7 2.0 %copy-start.1 = (f32[2048,512]{0,1:T(8,128)}, f32[2048,512]{0,1:T(8,128)S(1)}, u32[]{:S(2)}) copy-start(f32[2048,512]{0,1:T(8,128)S(1)} %maximum_add_fusion.2) | copy-start | bytes 12582916 | tf_op jit(solution)/shard_map/while
  20.3 4.9 %copy-start = (f32[2048,512]{0,1:T(8,128)S(1)}, f32[2048,512]{0,1:T(8,128)}, u32[]{:S(2)}) copy-start(f32[2048,512]{0,1:T(8,128)} %get-tuple-element.129) | copy-start | bytes 12582916 | tf_op jit(solution)/shard_map/while
  26.7 2.0 %copy-start.1 = (f32[2048,512]{0,1:T(8,128)}, f32[2048,512]{0,1:T(8,128)S(1)}, u32[]{:S(2)}) copy-start(f32[2048,512]{0,1:T(8,128)S(1)} %maximum_add_fusion.2) | copy-start | bytes 12582916 | tf_op jit(solution)/shard_map/while
  34.3 4.9 %copy-start = (f32[2048,512]{0,1:T(8,128)S(1)}, f32[2048,512]{0,1:T(8,128)}, u32[]{:S(2)}) copy-start(f32[2048,512]{0,1:T(8,128)} %get-tuple-element.129) | copy-start | bytes 12582916 | tf_op jit(solution)/shard_map/while
  40.7 2.0 %copy-start.1 = (f32[2048,512]{0,1:T(8,128)}, f32[2048,512]{0,1:T(8,128)S(1)}, u32[]{:S(2)}) copy-start(f32[2048,512]{0,1:T(8,128)S(1)} %maximum_add_fusion.2) | copy-start | bytes 12582916 | tf_op jit(solution)/shard_map/while
  48.3 4.9 %copy-start = (f32[2048,512]{0,1:T(8,128)S(1)}, f32[2048,512]{0,1:T(8,128)}, u32[]{:S(2)}) copy-start(f32[2048,512]{0,1:T(8,128)} %get-tuple-element.129) | copy-start | bytes 12582916 | tf_op jit(solution)/shard_map/while
  54.8 2.0 %copy-start.1 = (f32[2048,512]{0,1:T(8,128)}, f32[2048,512]{0,1:T(8,128)S(1)}, u32[]{:S(2)}) copy-start(f32[2048,512]{0,1:T(8,128)S(1)} %maximum_add_fusion.2) | copy-start | bytes 12582916 | tf_op jit(solution)/shard_map/while
  67.1 12.0 %copy-start.2 = (s32[2,128]{1,0:T(2,128)S(1)}, s32[2,128]{1,0:T(2,128)}, u32[]{:S(2)}) copy-start(s32[2,128]{1,0:T(2,128)} %param.9) | copy-start | bytes 3076
  67.1 63.1 %all-to-all-start = ((f32[128,16,512]{2,1,0:T(8,128)}), f32[128,16,512]{2,1,0:T(8,128)}, u32[]{:S(2)}, u32[]{:S(2)}) async-start(f32[128,16,512]{2,1,0:T(8,128)} %bitcast.62), calls=%async_computation | async-start | bytes 8388608 | tf_op jit(solution)/shard_map/all_to_all | solution.py:66
  79.2 50.2 %collective-permute-start.6 = (s32[16,2]{0,1:T(2,128)S(1)}, s32[16,2]{0,1:T(2,128)S(1)}, u32[]{:S(2)}, u32[]{:S(2)}) collective-permute-start(s32[16,2]{0,1:T(2,128)S(1)} %get-tuple-element.82), channel_id=1, source_target_pairs={{0,112},{16,96},{32,80},{48,64},{64,48},{80,32},{96,16},{112,0},{1... | collective-permute-start | bytes 392 | tf_op jit(solution)/shard_map/ppermute | solution.py:80
  82.1 44.5 %collective-permute-start.4 = (s32[16,2]{0,1:T(2,128)S(1)}, s32[16,2]{0,1:T(2,128)S(1)}, u32[]{:S(2)}, u32[]{:S(2)}) collective-permute-start(s32[16,2]{0,1:T(2,128)S(1)} %get-tuple-element.83), channel_id=1, source_target_pairs={{0,80},{16,64},{32,112},{48,96},{64,16},{80,0},{96,48},{112,32},{1... | collective-permute-start | bytes 392 | tf_op jit(solution)/shard_map/ppermute | solution.py:80
  82.7 43.7 %collective-permute-start.3 = (s32[16,2]{0,1:T(2,128)S(1)}, s32[16,2]{0,1:T(2,128)S(1)}, u32[]{:S(2)}, u32[]{:S(2)}) collective-permute-start(s32[16,2]{0,1:T(2,128)S(1)} %get-tuple-element.84), channel_id=1, source_target_pairs={{0,64},{16,80},{32,96},{48,112},{64,0},{80,16},{96,32},{112,48},{1... | collective-permute-start | bytes 392 | tf_op jit(solution)/shard_map/ppermute | solution.py:80
  85.1 39.9 %collective-permute-start.1 = (s32[16,2]{0,1:T(2,128)S(1)}, s32[16,2]{0,1:T(2,128)S(1)}, u32[]{:S(2)}, u32[]{:S(2)}) collective-permute-start(s32[16,2]{0,1:T(2,128)S(1)} %get-tuple-element.86), channel_id=1, source_target_pairs={{0,32},{16,48},{32,0},{48,16},{64,96},{80,112},{96,64},{112,80},{1... | collective-permute-start | bytes 392 | tf_op jit(solution)/shard_map/ppermute | solution.py:80
  85.1 1.6 %collective-permute-start = (s32[16,2]{0,1:T(2,128)S(1)}, s32[16,2]{0,1:T(2,128)S(1)}, u32[]{:S(2)}, u32[]{:S(2)}) collective-permute-start(s32[16,2]{0,1:T(2,128)S(1)} %get-tuple-element.87), channel_id=1, source_target_pairs={{0,16},{16,0},{32,48},{48,32},{64,80},{80,64},{96,112},{112,96},{1... | collective-permute-start | bytes 392 | tf_op jit(solution)/shard_map/ppermute | solution.py:80
  86.8 39.4 %collective-permute-start.2 = (s32[16,2]{0,1:T(2,128)S(1)}, s32[16,2]{0,1:T(2,128)S(1)}, u32[]{:S(2)}, u32[]{:S(2)}) collective-permute-start(s32[16,2]{0,1:T(2,128)S(1)} %get-tuple-element.85), channel_id=1, source_target_pairs={{0,48},{16,32},{32,16},{48,0},{64,112},{80,96},{96,80},{112,64},{1... | collective-permute-start | bytes 392 | tf_op jit(solution)/shard_map/ppermute | solution.py:80
  125.0 4.1 %collective-permute-start.5 = (s32[16,2]{0,1:T(2,128)S(1)}, s32[16,2]{0,1:T(2,128)S(1)}, u32[]{:S(2)}, u32[]{:S(2)}) collective-permute-start(s32[16,2]{0,1:T(2,128)S(1)} %get-tuple-element.89), channel_id=1, source_target_pairs={{0,96},{16,112},{32,64},{48,80},{64,32},{80,48},{96,0},{112,16},{1... | collective-permute-start | bytes 392 | tf_op jit(solution)/shard_map/ppermute | solution.py:80
  129.6 6.8 %copy-start.3 = (f32[2,1024]{1,0:T(2,128)S(1)}, f32[2,1024]{1,0:T(2,128)}, u32[]{:S(2)}) copy-start(f32[2,1024]{1,0:T(2,128)} %param.11) | copy-start | bytes 24580
